TPU v7x, 256 devices: a whole 4x4x8 slice. The times are simulated.
256 devices in a mesh: grid: 8 (over z), dom: 32 (over y, x, core).
Axes of the slice: x: 4, y: 4, z: 8, core: 2. Of those that a mesh axis runs over, the one named last changes fastest.
Arguments:
- nodal_values: float32 [16, 256, 8192], P('grid', None, 'dom'), may hold values from -6 to 6
- source_term: float32 [16, 256, 8192], P('grid', None, 'dom'), may hold values from -6 to 6
- velocity: float32 [16, 2], P('grid'), may hold values from 0.2 to 0.9
- react_rate: float32 [16], P('grid'), may hold values from 0.3 to 3
- levels: int32 [16, 2], P('grid'), may hold values from 5 to 8, as said below
- comb_coefs: int32 [16], P('grid'), may hold values from -1 to 1, as said below
Outputs:
- combined: float32 [16, 256, 8192], P('grid', None, 'dom')
Inputs may be any that keep to these rules, and one draw needn't show every extreme that they name: Each grid's two levels sum to 13 or 12. comb_coefs[c] is 1 where the levels of grid c sum to 13 and -1 where they sum to 12.
All inputs are finite; a program needn't handle non-finite values.
Results may differ from a plain program's by a relative error of at most 0.0003.
Values sent between devices are 32-bit elements; how exact they have to be, the bound alone decides.
A program may use at most 64 MiB of HBM per device.

v0:
```python
import jax
import jax.numpy as jnp
import numpy as np
from jax import lax
from jax.sharding import PartitionSpec as P

MAXL = 8
LINE = 256
LSUM = 13
MINL = 5


tau_react = 0.25


def fine_order(line_depth):
    listing = [0]
    for tier_num in range(1, line_depth + 1):
        stride_len = 2 ** (line_depth - tier_num)
        listing.extend(range(stride_len, 2**line_depth, 2 * stride_len))
    return np.array(listing, np.int32)


def column_slots(line_depth, lowest_level, level_sum, dom_count):
    shift_bits = dom_count.bit_length() - 1
    slot_limit = []
    for column in range(2**line_depth // dom_count):
        least_level = lowest_level
        if column > 0:
            least_level = max(lowest_level, column.bit_length() + shift_bits)
        slot_limit.append(2 ** min(line_depth, level_sum - least_level))
    slot_limit = np.array(slot_limit, np.int32)
    starts = np.concatenate([np.zeros(1, np.int32), np.cumsum(slot_limit)[:-1]]).astype(np.int32)
    owners = np.repeat(np.arange(slot_limit.shape[0], dtype=np.int32), slot_limit)
    return (starts, owners)


def select_table(place_idx, source_len, grid_count):
    sources = jnp.arange(source_len, dtype=jnp.int32)[None, :, None]
    onehot = (place_idx[:, None, :] == sources).astype(jnp.float32)
    return jnp.broadcast_to(onehot, (grid_count, source_len, place_idx.shape[-1]))


def pick_last(source_arr, place_idx):
    table = select_table(place_idx, source_arr.shape[-1], source_arr.shape[0])
    return jnp.einsum("zrs,zsd->zrd", source_arr, table, precision=lax.Precision.HIGHEST)


def advect_line(values, line_base, position, line_len, courant):
    ahead = pick_last(values, line_base + (position + 1) % line_len)
    behind = pick_last(values, line_base + (position + line_len - 1) % line_len)
    return (
        values
        - 0.5 * courant * (ahead - behind)
        + 0.5 * courant * courant * (ahead - 2.0 * values + behind)
    )


def hier_gather(values, line_base, position, line_len, line_level, order_table):
    node_idx = jnp.right_shift(jnp.take(order_table, position), MAXL - line_level)
    spacing = jnp.bitwise_and(node_idx, -node_idx)
    centre = pick_last(values, line_base + node_idx)
    left_val = pick_last(values, line_base + (node_idx - spacing) % line_len)
    right_val = pick_last(values, line_base + (node_idx + spacing) % line_len)
    half_w = jnp.where(node_idx > 0, 0.5, 0.0)[:, None, :]
    return centre - half_w * (left_val + right_val)


def hat_matrix(line_base, position, line_len, line_level, is_live, order_table):
    node_idx = jnp.right_shift(jnp.take(order_table, position), MAXL - line_level)
    spacing = jnp.bitwise_and(node_idx, -node_idx)
    apart = jnp.abs(position[:, :, None] - node_idx[:, None, :])
    apart = jnp.minimum(apart, line_len[:, :, None] - apart)
    ratio = apart.astype(jnp.float32) / jnp.maximum(spacing, 1).astype(jnp.float32)[:, None, :]
    weight = jnp.where(node_idx[:, None, :] == 0, 1.0, jnp.maximum(0.0, 1.0 - ratio))
    same_line = line_base[:, :, None] == line_base[:, None, :]
    both_live = is_live[:, :, None] & is_live[:, None, :]
    return jnp.where(same_line & both_live, weight, 0.0)


def combine_grids(partial_sum):
    return lax.psum(partial_sum, "grid")


def local(nodal_values, source_term, velocity, react_rate, levels, comb_coefs):
    grids_here, other_rows, block_len = nodal_values.shape
    dom_count = lax.axis_size("dom")
    segment = block_len // dom_count
    top_level_index = lax.Precision.HIGHEST
    order_table = jnp.asarray(fine_order(MAXL))
    start_np, owner_np = column_slots(MAXL, MINL, LSUM, dom_count)
    slot_starts = jnp.asarray(start_np)
    slot_owner = jnp.asarray(owner_np)[None, :]
    slot_offset = jnp.asarray(np.arange(owner_np.shape[0], dtype=np.int32) - start_np[owner_np])[
        None, :
    ]
    cols_level = levels[:, 0:1]
    rows_level = levels[:, 1:2]
    unit_ints = jnp.ones_like(cols_level)
    col_count = jnp.left_shift(unit_ints, cols_level)
    row_count = jnp.left_shift(unit_ints, rows_level)
    live_count = col_count * row_count // dom_count
    rows_block = live_count // col_count
    cols_block = col_count // dom_count
    places = jnp.arange(block_len, dtype=jnp.int32)[None, :]
    is_live = places < live_count
    live_mask = is_live.astype(jnp.float32)[:, None, :]
    nu_cols = (velocity[:, 0:1] * col_count.astype(jnp.float32) / LINE)[:, :, None]
    nu_rows = (velocity[:, 1:2] * row_count.astype(jnp.float32) / LINE)[:, :, None]
    row_local = places // col_count
    col_pos = places % col_count
    row_base = row_local * col_count
    col_local = places // row_count
    row_pos = places % row_count
    col_base = col_local * row_count
    dest_dev = places // segment
    slot_pos = places % segment
    send_ok = slot_pos < rows_block * cols_block
    send_mask = send_ok.astype(jnp.float32)[:, None, :]
    row_send = slot_pos // cols_block
    col_send = slot_pos % cols_block
    moved = nodal_values * live_mask
    moved = advect_line(moved, row_base, col_pos, col_count, nu_cols)
    reacted = (
        moved * (1.0 - tau_react * react_rate)[:, None, None] + tau_react * source_term * live_mask
    )
    surplus = hier_gather(reacted, row_base, col_pos, col_count, cols_level, order_table)
    send_from = jnp.where(send_ok, row_send * col_count + dest_dev + dom_count * col_send, 0)
    outgoing = (pick_last(surplus, send_from) * send_mask).reshape(
        grids_here, other_rows, dom_count, segment
    )
    incoming = lax.all_to_all(outgoing, "dom", split_axis=2, concat_axis=2, tiled=True).reshape(
        grids_here, other_rows, block_len
    )
    recv_from = jnp.where(
        is_live, row_pos // rows_block * segment + row_pos % rows_block * cols_block + col_local, 0
    )
    columns = pick_last(incoming, recv_from) * live_mask
    columns = advect_line(columns, col_base, row_pos, row_count, nu_rows)
    surplus = hier_gather(columns, col_base, row_pos, row_count, rows_level, order_table)
    pack_ok = (slot_owner < cols_block) & (slot_offset < row_count)
    pack_from = jnp.where(pack_ok, slot_owner * row_count + slot_offset, 0)
    pack_weight = (comb_coefs.astype(jnp.float32)[:, None] * pack_ok.astype(jnp.float32))[
        :, None, :
    ]
    partial_sum = jnp.sum(pick_last(surplus, pack_from) * pack_weight, axis=0)
    total_sum = combine_grids(partial_sum)
    unpack_at = jnp.where(
        is_live, jnp.take(slot_starts, jnp.where(is_live, col_local, 0)) + row_pos, 0
    )
    unpack_table = select_table(unpack_at, total_sum.shape[-1], grids_here)
    gathered_result = (
        jnp.einsum("rs,zsd->zrd", total_sum, unpack_table, precision=top_level_index) * live_mask
    )
    row_hat_values = hat_matrix(col_base, row_pos, row_count, rows_level, is_live, order_table)
    gathered_result = jnp.einsum(
        "zsd,zbd->zsb", gathered_result, row_hat_values, precision=top_level_index
    )
    gathered_result = advect_line(gathered_result, col_base, row_pos, row_count, nu_rows)
    send_back = jnp.where(send_ok, col_send * row_count + dest_dev * rows_block + row_send, 0)
    outgoing = (pick_last(gathered_result, send_back) * send_mask).reshape(
        grids_here, other_rows, dom_count, segment
    )
    incoming = lax.all_to_all(outgoing, "dom", split_axis=2, concat_axis=2, tiled=True).reshape(
        grids_here, other_rows, block_len
    )
    back_from = jnp.where(
        is_live, col_pos % dom_count * segment + row_local * cols_block + col_pos // dom_count, 0
    )
    row_arrangement = pick_last(incoming, back_from) * live_mask
    column_hat_values = hat_matrix(row_base, col_pos, col_count, cols_level, is_live, order_table)
    return jnp.einsum("zsd,zbd->zsb", row_arrangement, column_hat_values, precision=top_level_index)


def solution(mesh):
    in_specs = (
        P("grid", None, "dom"),
        P("grid", None, "dom"),
        P("grid", None),
        P("grid"),
        P("grid", None),
        P("grid"),
    )
    out_specs = P("grid", None, "dom")
    return jax.shard_map(local, mesh=mesh, in_specs=in_specs, out_specs=out_specs, check_vma=False)
```

profile of v0, /device:TPU:32, one launch (start us, length us, event | category | flops | bytes accessed | tf_op | source)
XLA Modules:
  0.0 157.0 jit_solution(4826393388266575318)
XLA Ops:
  6.6 1.1 compare_reduce_fusion.1
  7.9 1.0 multiply_reduce_fusion
  8.9 1.2 subtract_reduce_fusion
  10.6 3.3 %gather_fusion = s32[512]{0:T(512)S(1)} fusion(s32[8]{0:T(128)S(1)} %copy-done.1, s32[1024]{0:T(1024)S(1)} %pad_clamp_fusion.2), kind=kCustom, calls=%fused_computation.2 | custom fusion | bytes 6144 | tf_op jit(solution)/shard_map/jit(_take)/gather | solution.py:149
  14.2 3.5 %gather_fusion.1 = s32[512]{0:T(512)S(1)} fusion(s32[256]{0:T(256)S(1)} %copy-done, s32[1024]{0:T(1024)S(1)} %pad_clamp_fusion.1), kind=kCustom, calls=%fused_computation.clone | custom fusion | bytes 6144 | tf_op jit(solution)/shard_map/jit(_take)/gather | solution.py:60
  18.2 3.5 %gather_fusion.2 = s32[512]{0:T(512)S(1)} fusion(s32[256]{0:T(256)S(1)} %copy-done, s32[1024]{0:T(1024)S(1)} %pad_clamp_fusion), kind=kCustom, calls=%fused_computation.1.clone | custom fusion | bytes 6144 | tf_op jit(solution)/shard_map/jit(_take)/gather | solution.py:60
  22.0 1.3 fusion.122
  23.2 0.5 fusion.49
  23.7 0.6 multiply_add_fusion.1
  24.3 0.4 fusion.51
  24.8 0.4 fusion.50
  25.2 0.5 fusion.8
  25.7 0.5 fusion.6
  26.2 0.9 copy.19
  27.1 7.5 %all-to-all-start = ((f32[2,256,32,8]{1,3,0,2:T(8,128)}), f32[2,256,32,8]{1,3,0,2:T(8,128)S(1)}, u32[]{:S(2)}, u32[]{:S(2)}) async-start(f32[2,256,32,8]{1,3,0,2:T(8,128)} %copy.19), calls=%async_computation | async-start | bytes 1048576 | tf_op jit(solution)/shard_map/all_to_all | solution.py:132
  35.0 11.1 %all-to-all-done = f32[2,256,32,8]{1,3,0,2:T(8,128)S(1)} async-done(((f32[2,256,32,8]{1,3,0,2:T(8,128)}), f32[2,256,32,8]{1,3,0,2:T(8,128)S(1)}, u32[]{:S(2)}, u32[]{:S(2)}) %all-to-all-start) | async-done | bytes 524320 | tf_op jit(solution)/shard_map/all_to_all | solution.py:132
  46.1 0.6 convolution_multiply_fusion.3
  46.8 0.4 fusion.47
  47.2 0.5 multiply_add_fusion
  47.8 0.4 fusion.53
  48.2 0.4 fusion.52
  48.7 0.5 fusion.5
  49.1 1.8 %fusion = f32[256,640]{1,0:T(8,128)} fusion(f32[2,256,256]{2,1,0:T(8,128)S(1)} %fusion.5, f32[2,640]{1,0:T(2,128)S(1)} %broadcast_select_fusion, s32[2,640]{1,0:T(2,128)S(1)} %add_select_fusion), kind=kOutput, calls=%fused_computation.4 | convolution fusion | flops 1007452160 | bytes 1189888 | tf_op jit(solution)/shard_map/zrs,zsd->zrd/dot_general | solution.py:46
  50.9 73.2 %all-reduce.2.cloned.1.call-done = f32[256,640]{1,0:T(8,128)} async-done(((f32[256,640]{1,0:T(8,128)}), f32[256,640]{1,0:T(8,128)}) %all-reduce.2.cloned.1.call-update) | async-done | bytes 655376 | tf_op jit(solution)/shard_map/psum | solution.py:82
  124.1 2.0 %fusion.2 = f32[2,256,256]{2,1,0:T(8,128)S(1)} fusion(f32[256,640]{1,0:T(8,128)} %all-reduce.2.cloned.1.call-done, s32[2,256]{1,0:T(2,128)S(1)} %get-tuple-element.45, f32[2,256]{1,0:T(2,128)S(1)} %get-tuple-element.77), kind=kOutput, calls=%fused_computation.8 | convolution fusion | flops 1007091712 | bytes 1183744 | tf_op jit(solution)/shard_map/rs,zsd->zrd/dot_general | solution.py:153
  126.1 1.5 fusion.18
  127.6 0.4 fusion.44
  128.0 0.4 fusion.46
  128.5 0.7 fusion.3
  129.2 18.5 %all_to_all.10 = f32[2,256,32,8]{1,3,0,2:T(8,128)S(1)} all-to-all(f32[2,256,32,8]{1,3,0,2:T(8,128)S(1)} %copy.23), channel_id=1, replica_groups=mesh['grid'=8,'dom'=32] {'dom'}, dimensions={2} | all-to-all | bytes 1048576 | tf_op jit(solution)/shard_map/all_to_all | solution.py:164
  147.7 0.6 convolution_multiply_fusion.1
  148.3 1.8 %fusion.26 = f32[2,256,256]{2,1,0:T(8,128)} fusion(f32[2,256,256]{2,1,0:T(8,128)S(1)} %convolution_multiply_fusion.1, f32[2,256]{1,0:T(2,128)S(1)} %get-tuple-element.64, s32[2]{0:T(128)S(1)} %get-tuple-element.12, s32[2,256]{1,0:T(2,128)S(1)} %get-tuple-element.29, s32[2,256]{1,0:T(2,128)S(1)} %get-tuple-element.68, s32[2,256]{1,0:T(2,128)S(1)} %get-tuple-element.65, ...), kind=kOutput, calls=%fused_computation.41 | convolution fusion | flops 404357120 | bytes 1057800 | tf_op jit(solution)/shard_map/zsd,zbd->zsb/dot_general | solution.py:172
  (48 shorter events, 2.1 us)
Async XLA Ops:
  6.5 4.0 %copy-start.1 = (s32[8]{0:T(128)S(1)}, s32[8]{0:T(128)}, u32[]{:S(2)}) copy-start(s32[8]{0:T(128)} %constant.160.clone) | copy-start | bytes 100
  10.6 3.6 %copy-start = (s32[256]{0:T(256)S(1)}, s32[256]{0:T(256)}, u32[]{:S(2)}) copy-start(s32[256]{0:T(256)} %constant.159.clone2.2) | copy-start | bytes 3076
  18.2 3.6 %copy-start.6 = (f32[2]{0:T(128)S(1)}, f32[2]{0:T(128)}, u32[]{:S(2)}) copy-start(f32[2]{0:T(128)} %param.21) | copy-start | bytes 28
  18.2 5.0 %copy-start.2 = (f32[2,256,256]{2,1,0:T(8,128)S(1)}, f32[2,256,256]{2,1,0:T(8,128)}, u32[]{:S(2)}) copy-start(f32[2,256,256]{2,1,0:T(8,128)} %param.18) | copy-start | bytes 1572868
  21.7 2.0 %copy-start.3 = (f32[2,256,256]{2,1,0:T(8,128)S(1)}, f32[2,256,256]{2,1,0:T(8,128)}, u32[]{:S(2)}) copy-start(f32[2,256,256]{2,1,0:T(8,128)} %param.19) | copy-start | bytes 1572868
  27.0 7.7 %copy-start.7 = (s32[2]{0:T(128)S(1)}, s32[2]{0:T(128)}, u32[]{:S(2)}) copy-start(s32[2]{0:T(128)} %param.23) | copy-start | bytes 28
  27.0 7.7 %copy-start.4 = (s32[640]{0:T(1024)S(1)}, s32[640]{0:T(1024)}, u32[]{:S(2)}) copy-start(s32[640]{0:T(1024)} %constant.162.clone) | copy-start | bytes 7684
  27.0 7.8 %copy-start.5 = (s32[640]{0:T(1024)S(1)}, s32[640]{0:T(1024)}, u32[]{:S(2)}) copy-start(s32[640]{0:T(1024)} %constant.161.clone) | copy-start | bytes 7684
  27.1 19.1 %all-to-all-start = ((f32[2,256,32,8]{1,3,0,2:T(8,128)}), f32[2,256,32,8]{1,3,0,2:T(8,128)S(1)}, u32[]{:S(2)}, u32[]{:S(2)}) async-start(f32[2,256,32,8]{1,3,0,2:T(8,128)} %copy.19), calls=%async_computation | async-start | bytes 1048576 | tf_op jit(solution)/shard_map/all_to_all | solution.py:132
  34.5 89.6 %all-reduce.2.cloned.1.call-start = ((), (), s32[]{:S(2)}) async-start(), calls=%async_computation.2 | async-start | bytes 1310720 | tf_op jit(solution)/shard_map/psum | solution.py:82
Sparse Core Ops, SparseCore 0:
  51.0 73.0 all-reduce.1
where the time goes:
time: 159 us; the launch traced here: 157 us
  waiting for transfers between devices  84.3 us (53%)
  blocking collectives  18.5 us (12%)
  matrix products  15.1 us (9%)
  between operations  13.8 us (9%)
  local copies, waits for them, and re-layouts  11.4 us (7%)
  starting transfers between devices  7.68 us (5%)
  other arithmetic  6.23 us (4%)
    psum x1, waiting for transfers between devices, combine_grids(): return lax.psum(partial_sum, 'grid')  73.2 us
    all_to_all x1, blocking collectives, local(): lax.all_to_all(outgoing, 'dom', split_axis=2, concat_axis=2, tiled=True)  18.5 us
    all_to_all x1, waiting for transfers between devices, local(): lax.all_to_all(outgoing, 'dom', split_axis=2, concat_axis=2, tiled=True)  11.1 us
    dot_general x17, matrix products, pick_last(): jnp.einsum('zrs,zsd->zrd', source_arr, table, precision=lax.Precision.HIG...  9.85 us
    all_to_all x1, starting transfers between devices, local(): lax.all_to_all(outgoing, 'dom', split_axis=2, concat_axis=2, tiled=True)  7.45 us
    gather x4, local copies, waits for them, and re-layouts, hier_gather(): jnp.take(order_table, position)  7.04 us
    gather x2, local copies, waits for them, and re-layouts, local(): jnp.take(slot_starts, jnp.where(is_live, col_local, 0)) + row_pos  3.36 us
  transfers between devices with their start and end apart: 2, of which 2 were waited for; matrix products, arithmetic and copies ran while one was open for 0% of the time, Pallas kernels for 0%

commit v1 on v0

v1 whole, which is shorter than its diff:
```python
import functools

import jax
import jax.numpy as jnp
from jax import lax
from jax.experimental import pallas as pl
from jax.experimental.pallas import tpu as pltpu
from jax.sharding import PartitionSpec as P

TAU = 0.25
MESH = pl.DeviceIdType.MESH
BLOCKS = {2: (0, 2), 1: (2, 1), 0: (3, 8), 4: (11, 4), 6: (15, 2), 7: (17, 1), 3: (18, 1), 5: (19, 1)}
UP = (2, 1, 0, 4)
DOWN = (0, 4, 6, 7)
UP_ROWS = (0, 120)
DOWN_ROWS = (24, 120)
FIRST_ROWS = (24, 64)
QUARTERS = 4
FAR = 1 << 20
KDIM = 1280


def dot(left, right, dims):
    return lax.dot_general(left, right, (dims, ((), ())), preferred_element_type=jnp.float32)


def split(value):
    high = value.astype(jnp.bfloat16)
    return high, (value - high.astype(jnp.float32)).astype(jnp.bfloat16)


def stencil(courant):
    square = courant * courant
    return 1.0 - square, 0.5 * (square + courant), 0.5 * (square - courant)


def build_tables(grid, step, lv_ref, vel_ref, rate_ref, left_ref, hat_ref):
    lx, m = lv_ref[grid, 0], lv_ref[grid, 1] - 5
    cols = jnp.left_shift(1, lx)
    gap = jnp.left_shift(1, 8 - lx)
    keep = 1.0 - TAU * rate_ref[grid]
    centre, behind, ahead = stencil(vel_ref[grid, 0] * cols.astype(jnp.float32) * (1.0 / 256.0))
    centre, behind, ahead = keep * centre, keep * behind, keep * ahead

    q = lax.broadcasted_iota(jnp.int32, (32, 128), 0) + step * 32
    quarter = jnp.right_shift(q, 6)
    t = q & 63
    row = jnp.right_shift(t, 6 - m)
    j = t & (jnp.right_shift(64, m) - 1)
    place = 64 * quarter + jnp.where(
        j < 8, 8 * j, jnp.where(j < 16, 8 * j - 60, jnp.where(j < 32, 4 * j - 62, 2 * j - 63))
    )
    reach = jnp.where(j < 8, FAR, jnp.where(j < 16, 4, jnp.where(j < 32, 2, 1)))
    slope = jnp.where(j < 8, 0.125, jnp.where(j < 16, 0.25, jnp.where(j < 32, 0.5, 1.0)))
    row_key = jnp.left_shift(jnp.where(j < jnp.right_shift(cols, 2), row, 1 << 12), 8)
    past = 256 - reach + gap
    past = jnp.where(past == 256, 0, past)
    rows = pl.ds(pl.multiple_of(step * 32, 32), 32)
    for half in range(2):
        p = lax.broadcasted_iota(jnp.int32, (1, 128), 1) + 128 * half
        at = jnp.left_shift(p & (cols - 1), 8 - lx)
        key = jnp.left_shift(jnp.right_shift(p, lx), 8)
        other = key ^ row_key
        apart = (at - place) & 255
        delta = apart | other

        def pick(target, weight):
            return jnp.where(delta == target, weight, 0.0)

        here, right, left = delta == 0, delta == reach, delta == 256 - reach
        tree = jnp.where(here, 1.0, 0.0) - jnp.where(right, 0.5, 0.0) - jnp.where(left, 0.5, 0.0)
        full = (
            centre * tree
            + behind * (pick(256 - gap, 1.0) - pick(reach - gap, 0.5) - pick(256 - reach - gap, 0.5))
            + ahead * (pick(gap, 1.0) - pick(reach + gap, 0.5) - pick(past, 0.5))
        )
        high, low = split(full)
        quart = (TAU * tree).astype(jnp.bfloat16)
        for slot, table in enumerate((high, high, low, quart, quart)):
            left_ref[grid, rows, slot * 256 + half * 128 : slot * 256 + half * 128 + 128] = table
        near = jnp.minimum(apart, 256 - apart).astype(jnp.float32)
        hat = jnp.where(other == 0, jnp.maximum(0.0, 1.0 - near * slope), 0.0).astype(jnp.bfloat16)
        lanes = slice(half * 128, half * 128 + 128)
        hat_ref[grid, rows, lanes] = hat
        hat_ref[grid, pl.ds(pl.multiple_of(256 + step * 32, 32), 32), lanes] = hat


def class_weights(grid, lv_ref, vel_ref, scale):
    m = lv_ref[grid, 1] - 5
    rows = jnp.left_shift(1, m).astype(jnp.float32)
    weights = stencil(vel_ref[grid, 1] * rows * 0.125)
    return [[jnp.where(m == c, scale * w, 0.0) for w in weights] for c in range(4)]


class Sums:
    def __init__(self):
        self.held = {}

    def add(self, offset, number, value):
        key = (offset, number)
        self.held[key] = value if key not in self.held else self.held[key] + value


def spread(blocks, weights, own, up, down):
    for c in range(4):
        centre, behind, ahead = weights[c]
        count = 1 << c
        per = 8 >> c
        for n in range(per):
            w = [blocks[k * per + n] for k in range(count)]
            moved = []
            for k in range(count):
                value = centre * w[k]
                if k > 0:
                    value += behind * w[k - 1]
                if k < count - 1:
                    value += ahead * w[k + 1]
                moved.append(value)
            above, below = behind * w[-1], ahead * w[0]
            line = moved + [above]
            own.add(0, n, moved[0])
            up.add(0, n, above)
            if count == 1:
                down.add(0, n, below)
            for k in range(1, count):
                s = k & -k
                own.add(k * 8 // count, n, line[k] - 0.5 * (line[k - s] + line[k + s]))
            level = 2
            while level <= count:
                up.add(8 // level, n, -0.5 * above)
                spill = -0.5 * moved[0]
                if level == count:
                    spill += below
                down.add(8 - 8 // level, n, spill)
                level *= 2


def contribute(chunk, lv_ref, vel_ref, coef_ref, w_ref, total_ref, up_ref, down_ref):
    half, quarter = chunk // QUARTERS, chunk % QUARTERS
    own, up, down = Sums(), Sums(), Sums()
    for grid in range(2):
        weights = class_weights(grid, lv_ref, vel_ref, coef_ref[grid].astype(jnp.float32))
        blocks = [
            w_ref[grid, half, pl.ds(pl.multiple_of(quarter * 64 + 8 * n, 8), 8), :] for n in range(8)
        ]
        spread(blocks, weights, own, up, down)
    for offset, (start, count) in BLOCKS.items():
        for n in range(count):
            at = 8 * (start + n)
            total_ref[chunk, at : at + 8, :] = own.held[offset, n]
            if offset in UP:
                up_ref[chunk, at - UP_ROWS[0] : at - UP_ROWS[0] + 8, :] = up.held[offset, n]
            if offset in DOWN:
                down_ref[chunk, at - DOWN_ROWS[0] : at - DOWN_ROWS[0] + 8, :] = down.held[offset, n]


def interpolate(chunk, lv_ref, vel_ref, all_ref, prev_ref, next_ref, g_ref):
    half, quarter = chunk // QUARTERS, chunk % QUARTERS

    def held(offset, n):
        at = 8 * (BLOCKS[offset][0] + n)
        return all_ref[chunk, at : at + 8, :]

    def before(offset, n):
        at = 8 * (BLOCKS[offset][0] + n) - DOWN_ROWS[0]
        return prev_ref[chunk, at : at + 8, :]

    weights = [class_weights(grid, lv_ref, vel_ref, 1.0) for grid in range(2)]
    sums = [Sums(), Sums()]
    for n in range(8):
        node = {0: held(0, n), 8: next_ref[chunk, 8 * n : 8 * n + 8, :]}
        back = {1: before(0, n)}
        last = back[1]
        for c in range(1, 4):
            if n >= 8 >> c:
                break
            s = 8 >> c
            for k in range(1, 1 << c, 2):
                node[k * s] = held(k * s, n) + 0.5 * (node[k * s - s] + node[k * s + s])
            last = before(8 - s, n) + 0.5 * (last + node[0])
            back[1 << c] = last
        for c in range(4):
            per = 8 >> c
            if n >= per:
                break
            count = 1 << c
            line = [back[count]] + [node[k * per] for k in range(count + 1)]
            for k in range(count):
                for grid in range(2):
                    centre, behind, ahead = weights[grid][c]
                    sums[grid].add(
                        0, k * per + n, centre * line[k + 1] + behind * line[k] + ahead * line[k + 2]
                    )
    for grid in range(2):
        for n in range(8):
            at = pl.ds(pl.multiple_of(quarter * 64 + 8 * n, 8), 8)
            g_ref[grid, half, at, :] = sums[grid].held[0, n]


def kernel(
    nz, nd,
    lv_ref, vel_ref, rate_ref, coef_ref, v_hbm, s_hbm, out_hbm,
    v_ref, s_ref, left_ref, right_ref, hat_ref, w_ref,
    total_ref, up_ref, down_ref, up_in, down_in, minus_in, plus_in,
    all_ref, prev_ref, next_ref, g_ref, out_ref,
    load_sem, store_sem, up_sem, down_sem, minus_sem, plus_sem, gminus_sem, gplus_sem, prev_sem, next_sem,
):
    z, d = lax.axis_index("grid"), lax.axis_index("dom")
    north, south = (lax.rem(z + 1, nz), d), (lax.rem(z + nz - 1, nz), d)
    after, ahead_of = (z, lax.rem(d + 1, nd)), (z, lax.rem(d + nd - 1, nd))
    loads = []
    for grid in range(2):
        for n, (source, target) in enumerate(((v_hbm, v_ref), (s_hbm, s_ref))):
            loads.append(pltpu.make_async_copy(source.at[grid], target.at[grid], load_sem.at[grid, n]))
            loads[-1].start()

    barrier = pltpu.get_barrier_semaphore()
    for peer in (north, south, after, ahead_of):
        pl.semaphore_signal(barrier, inc=1, device_id=peer, device_id_type=MESH)

    def remote(source, target, sems, slot, peer):
        return pltpu.make_async_remote_copy(
            src_ref=source, dst_ref=target, send_sem=sems.at[0, slot], recv_sem=sems.at[1, slot],
            device_id=peer, device_id_type=MESH,
        )

    for grid in range(2):
        @pl.loop(0, 8)
        def _(step):
            build_tables(grid, step, lv_ref, vel_ref, rate_ref, left_ref, hat_ref)

    for grid in range(2):
        loads[2 * grid].wait()
        loads[2 * grid + 1].wait()
        vh, vl = split(v_ref[grid])
        sh, sl = split(s_ref[grid])
        for slot, part in enumerate((vh, vl, vh, sh, sl)):
            right_ref[grid, :, slot * 256 : slot * 256 + 256] = part
        w = dot(left_ref[grid], right_ref[grid], ((1,), (1,)))
        w_ref[grid, 0] = w[:, :128]
        w_ref[grid, 1] = w[:, 128:]

    pl.semaphore_wait(barrier, 4)

    def up_copy(chunk):
        return remote(up_ref.at[chunk], up_in.at[chunk], up_sem, chunk, after)

    def down_copy(chunk):
        return remote(down_ref.at[chunk], down_in.at[chunk], down_sem, chunk, ahead_of)

    far = nz // 2

    @pl.loop(0, nz)
    def _(i):
        off = jnp.where(i % 2 == 0, nz - far + i // 2, far - 1 - (i - 1) // 2)
        chunk = lax.rem(z + off, nz)
        contribute(chunk, lv_ref, vel_ref, coef_ref, w_ref, total_ref, up_ref, down_ref)
        up_copy(chunk).start()
        down_copy(chunk).start()

    def gather_in(chunk, *others):
        up_copy(chunk).wait_recv()
        down_copy(chunk).wait_recv()
        u, w, x = UP_ROWS[1], DOWN_ROWS[0], DOWN_ROWS[0] + DOWN_ROWS[1]
        parts = [o[...] for o in others]

        def at(low, high, value):
            for o in others:
                value = value + o[low:high, :]
            return value

        total_ref[chunk, 0:w, :] = at(0, w, total_ref[chunk, 0:w, :] + up_in[chunk, 0:w, :])
        total_ref[chunk, w:u, :] = at(
            w, u, total_ref[chunk, w:u, :] + up_in[chunk, w:u, :] + down_in[chunk, 0 : u - w, :]
        )
        total_ref[chunk, u:x, :] = at(u, x, total_ref[chunk, u:x, :] + down_in[chunk, u - w : x - w, :])
        if others:
            total_ref[chunk, x:160, :] = at(x, 160, total_ref[chunk, x:160, :])

    def minus_copy(chunk, t):
        return remote(total_ref.at[chunk], minus_in.at[t], minus_sem, t, south)

    def plus_copy(chunk, t):
        return remote(total_ref.at[chunk], plus_in.at[t], plus_sem, t, north)

    for t in range(far):
        chunk = lax.rem(z + nz - far + t, nz)
        if t == 0:
            gather_in(chunk)
        else:
            minus_copy(chunk, t - 1).wait_recv()
            gather_in(chunk, minus_in.at[t - 1])
        minus_copy(chunk, t).start()
        if t < far - 1:
            chunk = lax.rem(z + far - 1 - t, nz)
            if t == 0:
                gather_in(chunk)
            else:
                plus_copy(chunk, t - 1).wait_recv()
                gather_in(chunk, plus_in.at[t - 1])
            plus_copy(chunk, t).start()
    minus_copy(z, far - 1).wait_recv()
    plus_copy(z, far - 2).wait_recv()
    gather_in(z, minus_in.at[far - 1], plus_in.at[far - 2])

    def prev_copy(chunk, source):
        return remote(
            source.at[chunk, DOWN_ROWS[0] : DOWN_ROWS[0] + DOWN_ROWS[1], :], prev_ref.at[chunk], prev_sem, chunk, after
        )

    def next_copy(chunk, source):
        return remote(
            source.at[chunk, FIRST_ROWS[0] : FIRST_ROWS[0] + FIRST_ROWS[1], :], next_ref.at[chunk], next_sem, chunk,
            ahead_of,
        )

    def gminus_copy(chunk, t, source):
        return remote(source.at[chunk], all_ref.at[chunk], gminus_sem, t, south)

    def gplus_copy(chunk, t, source):
        return remote(source.at[chunk], all_ref.at[chunk], gplus_sem, t, north)

    gminus_copy(z, 0, total_ref).start()
    gplus_copy(z, 0, total_ref).start()
    prev_copy(z, total_ref).start()
    next_copy(z, total_ref).start()
    all_ref[z] = total_ref[z]
    for t in range(1, far + 1):
        chunk = lax.rem(z + t, nz)
        gminus_copy(chunk, t - 1, all_ref).wait_recv()
        if t < far:
            gminus_copy(chunk, t, all_ref).start()
        prev_copy(chunk, all_ref).start()
        next_copy(chunk, all_ref).start()
        if t < far:
            chunk = lax.rem(z + nz - t, nz)
            gplus_copy(chunk, t - 1, all_ref).wait_recv()
            if t < far - 1:
                gplus_copy(chunk, t, all_ref).start()
            prev_copy(chunk, all_ref).start()
            next_copy(chunk, all_ref).start()

    @pl.loop(0, nz)
    def _(i):
        off = jnp.where(i % 2 == 0, nz - i // 2, (i + 1) // 2)
        chunk = lax.rem(z + off, nz)
        prev_copy(chunk, all_ref).wait_recv()
        next_copy(chunk, all_ref).wait_recv()
        interpolate(chunk, lv_ref, vel_ref, all_ref, prev_ref, next_ref, g_ref)

    stores = []
    for half in range(2):
        for grid in range(2):
            turned = jnp.transpose(g_ref[grid, half])
            high, low = split(turned)
            lanes = jnp.concatenate([high, low], axis=1)
            out_ref[grid, half * 128 : half * 128 + 128, :] = dot(lanes, hat_ref[grid], ((1,), (0,)))
            rows = slice(half * 128, half * 128 + 128)
            stores.append(
                pltpu.make_async_copy(
                    out_ref.at[grid, rows, :], out_hbm.at[grid, rows, :], store_sem.at[grid, half]
                )
            )
            stores[-1].start()

    @pl.loop(0, nz)
    def _(chunk):
        up_copy(chunk).wait_send()
        down_copy(chunk).wait_send()
        prev_copy(chunk, all_ref).wait_send()
        next_copy(chunk, all_ref).wait_send()

    for t in range(far):
        minus_copy(0, t).wait_send()
        gminus_copy(0, t, all_ref).wait_send()
        if t < far - 1:
            plus_copy(0, t).wait_send()
            gplus_copy(0, t, all_ref).wait_send()
    for store in stores:
        store.wait()


def local(nz, nd, nodal_values, source_term, velocity, react_rate, levels, comb_coefs):
    far = nz // 2
    f32, bf16 = jnp.float32, jnp.bfloat16
    smem = pl.BlockSpec(memory_space=pltpu.SMEM)
    hbm = pl.BlockSpec(memory_space=pl.ANY)
    sem = pltpu.SemaphoreType.DMA
    return pl.pallas_call(
        functools.partial(kernel, nz, nd),
        out_shape=jax.ShapeDtypeStruct((2, 256, 256), f32),
        in_specs=[smem, smem, smem, smem, hbm, hbm],
        out_specs=hbm,
        scratch_shapes=[
            pltpu.VMEM((2, 256, 256), f32),
            pltpu.VMEM((2, 256, 256), f32),
            pltpu.VMEM((2, 256, KDIM), bf16),
            pltpu.VMEM((2, 256, KDIM), bf16),
            pltpu.VMEM((2, 512, 256), bf16),
            pltpu.VMEM((2, 2, 256, 128), f32),
            pltpu.VMEM((nz, 160, 128), f32),
            pltpu.VMEM((nz, 120, 128), f32),
            pltpu.VMEM((nz, 120, 128), f32),
            pltpu.VMEM((nz, 120, 128), f32),
            pltpu.VMEM((nz, 120, 128), f32),
            pltpu.VMEM((far, 160, 128), f32),
            pltpu.VMEM((far - 1, 160, 128), f32),
            pltpu.VMEM((nz, 160, 128), f32),
            pltpu.VMEM((nz, 120, 128), f32),
            pltpu.VMEM((nz, 64, 128), f32),
            pltpu.VMEM((2, 2, 256, 128), f32),
            pltpu.VMEM((2, 256, 256), f32),
            sem((2, 2)),
            sem((2, 2)),
            sem((2, nz)),
            sem((2, nz)),
            sem((2, far)),
            sem((2, far)),
            sem((2, far)),
            sem((2, far)),
            sem((2, nz)),
            sem((2, nz)),
        ],
        compiler_params=pltpu.CompilerParams(collective_id=0, has_side_effects=True, vmem_limit_bytes=32 << 20),
    )(levels, velocity, react_rate, comb_coefs, nodal_values, source_term)


def solution(mesh):
    in_specs = (
        P("grid", None, "dom"),
        P("grid", None, "dom"),
        P("grid", None),
        P("grid"),
        P("grid", None),
        P("grid"),
    )
    body = functools.partial(local, mesh.shape["grid"], mesh.shape["dom"])
    return jax.shard_map(body, mesh=mesh, in_specs=in_specs, out_specs=P("grid", None, "dom"), check_vma=False)
```

time: 159 us -> 54.6 us (0.34)
  the two profiles are of different devices: /device:TPU:32 before, /device:TPU:7 now
where the time goes in v1:
time: 54.6 us; the launch traced here: 54.3 us
  Pallas kernels  48.8 us (89%)
  local copies, waits for them, and re-layouts  5.54 us (10%)
    pallas_call x1, Pallas kernels, local(): pl.pallas_call(functools.partial(kernel, nz, nd), out_shape=jax.ShapeDtyp...  48.8 us
    unnamed x13, local copies, waits for them, and re-layouts  5.54 us

profile of v1, /device:TPU:7, one launch (start us, length us, event | category | flops | bytes accessed | tf_op | source)
XLA Modules:
  0.0 54.3 jit_solution(10361577004174827495)
XLA Ops:
  0.0 0.0 copy-start
  0.0 1.0 %copy-done = f32[2,256,256]{2,1,0:T(8,128)S(1)} copy-done((f32[2,256,256]{2,1,0:T(8,128)S(1)}, f32[2,256,256]{2,1,0:T(8,128)}, u32[]{:S(2)}) %copy-start) | copy-done | bytes 524312
  1.0 0.0 copy-start.1
  1.0 1.0 %copy-done.1 = f32[2,256,256]{2,1,0:T(8,128)S(1)} copy-done((f32[2,256,256]{2,1,0:T(8,128)S(1)}, f32[2,256,256]{2,1,0:T(8,128)}, u32[]{:S(2)}) %copy-start.1) | copy-done | bytes 524312
  2.1 0.0 copy-start.2
  2.1 0.7 %copy-done.2 = s32[2,2]{1,0:T(2,128)S(1)} copy-done((s32[2,2]{1,0:T(2,128)S(1)}, s32[2,2]{1,0:T(2,128)}, u32[]{:S(2)}) %copy-start.2) | copy-done | bytes 40
  2.8 0.0 copy-start.3
  2.8 0.7 %copy-done.3 = f32[2,2]{1,0:T(2,128)S(1)} copy-done((f32[2,2]{1,0:T(2,128)S(1)}, f32[2,2]{1,0:T(2,128)}, u32[]{:S(2)}) %copy-start.3) | copy-done | bytes 40
  3.4 0.0 copy-start.4
  3.4 0.7 %copy-done.4 = f32[2]{0:T(128)S(1)} copy-done((f32[2]{0:T(128)S(1)}, f32[2]{0:T(128)}, u32[]{:S(2)}) %copy-start.4) | copy-done | bytes 32
  4.1 0.0 copy-start.5
  4.1 0.7 %copy-done.5 = s32[2]{0:T(128)S(1)} copy-done((s32[2]{0:T(128)S(1)}, s32[2]{0:T(128)}, u32[]{:S(2)}) %copy-start.5) | copy-done | bytes 32
  4.8 48.8 %shard_map.64 = f32[2,256,256]{2,1,0:T(8,128)S(1)} custom-call(s32[2,2]{1,0:T(2,128)S(1)} %copy-done.2, f32[2,2]{1,0:T(2,128)S(1)} %copy-done.3, f32[2]{0:T(128)S(1)} %copy-done.4, s32[2]{0:T(128)S(1)} %copy-done.5, f32[2,256,256]{2,1,0:T(8,128)S(1)} %copy-done, f32[2,256,256]{2,1,0:T(8,128)S(1)} %copy-done.1), custom_call_target="tpu_custom_call" | custom-call | tf_op jit(solution)/shard_map/pallas_call | solution.py:389
  53.5 0.8 %copy.8 = f32[2,256,256]{2,1,0:T(8,128)} copy(f32[2,256,256]{2,1,0:T(8,128)S(1)} %shard_map.64) | data formatting | bytes 1048576
Async XLA Ops:
  0.0 1.0 %copy-start = (f32[2,256,256]{2,1,0:T(8,128)S(1)}, f32[2,256,256]{2,1,0:T(8,128)}, u32[]{:S(2)}) copy-start(f32[2,256,256]{2,1,0:T(8,128)} %v_hbm.1) | copy-start | bytes 1572868
  1.0 1.0 %copy-start.1 = (f32[2,256,256]{2,1,0:T(8,128)S(1)}, f32[2,256,256]{2,1,0:T(8,128)}, u32[]{:S(2)}) copy-start(f32[2,256,256]{2,1,0:T(8,128)} %s_hbm.1) | copy-start | bytes 1572868
  2.1 0.7 %copy-start.2 = (s32[2,2]{1,0:T(2,128)S(1)}, s32[2,2]{1,0:T(2,128)}, u32[]{:S(2)}) copy-start(s32[2,2]{1,0:T(2,128)} %lv_ref.1) | copy-start | bytes 52
  2.8 0.7 %copy-start.3 = (f32[2,2]{1,0:T(2,128)S(1)}, f32[2,2]{1,0:T(2,128)}, u32[]{:S(2)}) copy-start(f32[2,2]{1,0:T(2,128)} %vel_ref.1) | copy-start | bytes 52
  3.4 0.7 %copy-start.4 = (f32[2]{0:T(128)S(1)}, f32[2]{0:T(128)}, u32[]{:S(2)}) copy-start(f32[2]{0:T(128)} %rate_ref.1) | copy-start | bytes 28
  4.1 0.7 %copy-start.5 = (s32[2]{0:T(128)S(1)}, s32[2]{0:T(128)}, u32[]{:S(2)}) copy-start(s32[2]{0:T(128)} %coef_ref.1) | copy-start | bytes 28

commit v2 on v1

--- a/solution.py
+++ b/solution.py
@@ -199,15 +199,23 @@
 
 def kernel(
     nz, nd,
-    lv_ref, vel_ref, rate_ref, coef_ref, v_hbm, s_hbm, out_hbm,
-    v_ref, s_ref, left_ref, right_ref, hat_ref, w_ref,
+    lv_hbm, vel_hbm, rate_hbm, coef_hbm, v_hbm, s_hbm, out_hbm,
+    lv_ref, vel_ref, rate_ref, coef_ref, v_ref, s_ref, left_ref, right_ref, hat_ref, w_ref,
     total_ref, up_ref, down_ref, up_in, down_in, minus_in, plus_in,
     all_ref, prev_ref, next_ref, g_ref, out_ref,
-    load_sem, store_sem, up_sem, down_sem, minus_sem, plus_sem, gminus_sem, gplus_sem, prev_sem, next_sem,
+    small_sem, load_sem, store_sem, up_sem, down_sem, minus_sem, plus_sem, gminus_sem, gplus_sem, prev_sem, next_sem,
 ):
     z, d = lax.axis_index("grid"), lax.axis_index("dom")
     north, south = (lax.rem(z + 1, nz), d), (lax.rem(z + nz - 1, nz), d)
     after, ahead_of = (z, lax.rem(d + 1, nd)), (z, lax.rem(d + nd - 1, nd))
+    small = [
+        pltpu.make_async_copy(source, target, small_sem.at[n])
+        for n, (source, target) in enumerate(
+            ((lv_hbm, lv_ref), (vel_hbm, vel_ref), (rate_hbm, rate_ref), (coef_hbm, coef_ref))
+        )
+    ]
+    for copy in small:
+        copy.start()
     loads = []
     for grid in range(2):
         for n, (source, target) in enumerate(((v_hbm, v_ref), (s_hbm, s_ref))):
@@ -224,6 +232,8 @@
             device_id=peer, device_id_type=MESH,
         )
 
+    for copy in small:
+        copy.wait()
     for grid in range(2):
         @pl.loop(0, 8)
         def _(step):
@@ -262,7 +272,6 @@
         up_copy(chunk).wait_recv()
         down_copy(chunk).wait_recv()
         u, w, x = UP_ROWS[1], DOWN_ROWS[0], DOWN_ROWS[0] + DOWN_ROWS[1]
-        parts = [o[...] for o in others]
 
         def at(low, high, value):
             for o in others:
@@ -383,15 +392,18 @@
 def local(nz, nd, nodal_values, source_term, velocity, react_rate, levels, comb_coefs):
     far = nz // 2
     f32, bf16 = jnp.float32, jnp.bfloat16
-    smem = pl.BlockSpec(memory_space=pltpu.SMEM)
     hbm = pl.BlockSpec(memory_space=pl.ANY)
     sem = pltpu.SemaphoreType.DMA
     return pl.pallas_call(
         functools.partial(kernel, nz, nd),
         out_shape=jax.ShapeDtypeStruct((2, 256, 256), f32),
-        in_specs=[smem, smem, smem, smem, hbm, hbm],
+        in_specs=[hbm] * 6,
         out_specs=hbm,
         scratch_shapes=[
+            pltpu.SMEM((2, 2), jnp.int32),
+            pltpu.SMEM((2, 2), f32),
+            pltpu.SMEM((2,), f32),
+            pltpu.SMEM((2,), jnp.int32),
             pltpu.VMEM((2, 256, 256), f32),
             pltpu.VMEM((2, 256, 256), f32),
             pltpu.VMEM((2, 256, KDIM), bf16),
@@ -410,6 +422,7 @@
             pltpu.VMEM((nz, 64, 128), f32),
             pltpu.VMEM((2, 2, 256, 128), f32),
             pltpu.VMEM((2, 256, 256), f32),
+            sem((4,)),
             sem((2, 2)),
             sem((2, 2)),
             sem((2, nz)),
@@ -421,7 +434,7 @@
             sem((2, nz)),
             sem((2, nz)),
         ],
-        compiler_params=pltpu.CompilerParams(collective_id=0, has_side_effects=True, vmem_limit_bytes=32 << 20),
+        compiler_params=pltpu.CompilerParams(collective_id=0, has_side_effects=True, vmem_limit_bytes=67043328),
     )(levels, velocity, react_rate, comb_coefs, nodal_values, source_term)
 
 

time: 54.6 us -> 48.6 us (0.89)
  the two profiles are of different devices: /device:TPU:7 before, /device:TPU:1 now
where the time goes in v2:
time: 48.6 us; the launch traced here: 48.4 us
  Pallas kernels  46.6 us (96%)
  local copies, waits for them, and re-layouts  1.87 us (4%)
    pallas_call x1, Pallas kernels, local(): pl.pallas_call(functools.partial(kernel, nz, nd), out_shape=jax.ShapeDtyp...  46.6 us
    unnamed x1, local copies, waits for them, and re-layouts  1.87 us

profile of v2, /device:TPU:1, one launch (start us, length us, event | category | flops | bytes accessed | tf_op | source)
XLA Modules:
  0.0 48.4 jit_solution(11493120710186977970)
XLA Ops:
  0.0 46.6 %shard_map.64 = f32[2,256,256]{2,1,0:T(8,128)} custom-call(s32[2,2]{1,0:T(2,128)} %lv_hbm.1, f32[2,2]{1,0:T(2,128)} %vel_hbm.1, f32[2]{0:T(128)} %rate_hbm.1, s32[2]{0:T(128)} %coef_hbm.1, f32[2,256,256]{2,1,0:T(8,128)} %v_hbm.1, f32[2,256,256]{2,1,0:T(8,128)} %s_hbm.1), custom_call_target="tpu_custom_call" | custom-call | tf_op jit(solution)/shard_map/pallas_call | solution.py:397
  46.6 1.9 %copy.8 = f32[2,256,256]{2,1,0:T(8,128)} copy(f32[2,256,256]{2,1,0:T(8,128)} %shard_map.64) | data formatting | bytes 1048576

commit v3 on v2

v3 whole, which is shorter than its diff:
```python
import functools

import jax
import jax.numpy as jnp
from jax import lax
from jax.experimental import pallas as pl
from jax.experimental.pallas import tpu as pltpu
from jax.sharding import PartitionSpec as P

TAU = 0.25
MESH = pl.DeviceIdType.MESH
BLOCKS = {2: (0, 2), 1: (2, 1), 0: (3, 8), 4: (11, 4), 6: (15, 2), 7: (17, 1), 3: (18, 1), 5: (19, 1)}
UP = (2, 1, 0, 4)
DOWN = (0, 4, 6, 7)
UP_ROWS = (0, 120)
DOWN_ROWS = (24, 120)
QUARTERS = 4
FAR = 1 << 20
KDIM = 1280


def dot(left, right, dims):
    return lax.dot_general(left, right, (dims, ((), ())), preferred_element_type=jnp.float32)


def split(value):
    high = value.astype(jnp.bfloat16)
    return high, (value - high.astype(jnp.float32)).astype(jnp.bfloat16)


def stencil(courant):
    square = courant * courant
    return 1.0 - square, 0.5 * (square + courant), 0.5 * (square - courant)


def build_tables(grid, step, lv_ref, vel_ref, rate_ref, left_ref, hat_ref):
    lx, m = lv_ref[grid, 0], lv_ref[grid, 1] - 5
    cols = jnp.left_shift(1, lx)
    gap = jnp.left_shift(1, 8 - lx)
    keep = 1.0 - TAU * rate_ref[grid]
    centre, behind, ahead = stencil(vel_ref[grid, 0] * cols.astype(jnp.float32) * (1.0 / 256.0))
    centre, behind, ahead = keep * centre, keep * behind, keep * ahead

    q = lax.broadcasted_iota(jnp.int32, (32, 128), 0) + step * 32
    quarter = jnp.right_shift(q, 6)
    t = q & 63
    row = jnp.right_shift(t, 6 - m)
    j = t & (jnp.right_shift(64, m) - 1)
    place = 64 * quarter + jnp.where(
        j < 8, 8 * j, jnp.where(j < 16, 8 * j - 60, jnp.where(j < 32, 4 * j - 62, 2 * j - 63))
    )
    reach = jnp.where(j < 8, FAR, jnp.where(j < 16, 4, jnp.where(j < 32, 2, 1)))
    slope = jnp.where(j < 8, 0.125, jnp.where(j < 16, 0.25, jnp.where(j < 32, 0.5, 1.0)))
    row_key = jnp.left_shift(jnp.where(j < jnp.right_shift(cols, 2), row, 1 << 12), 8)
    past = 256 - reach + gap
    past = jnp.where(past == 256, 0, past)
    rows = pl.ds(pl.multiple_of(step * 32, 32), 32)
    for half in range(2):
        p = lax.broadcasted_iota(jnp.int32, (1, 128), 1) + 128 * half
        at = jnp.left_shift(p & (cols - 1), 8 - lx)
        key = jnp.left_shift(jnp.right_shift(p, lx), 8)
        other = key ^ row_key
        apart = (at - place) & 255
        delta = apart | other

        def pick(target, weight):
            return jnp.where(delta == target, weight, 0.0)

        here, right, left = delta == 0, delta == reach, delta == 256 - reach
        tree = jnp.where(here, 1.0, 0.0) - jnp.where(right, 0.5, 0.0) - jnp.where(left, 0.5, 0.0)
        full = (
            centre * tree
            + behind * (pick(256 - gap, 1.0) - pick(reach - gap, 0.5) - pick(256 - reach - gap, 0.5))
            + ahead * (pick(gap, 1.0) - pick(reach + gap, 0.5) - pick(past, 0.5))
        )
        high, low = split(full)
        quart = (TAU * tree).astype(jnp.bfloat16)
        for slot, table in enumerate((high, high, low, quart, quart)):
            left_ref[grid, rows, slot * 256 + half * 128 : slot * 256 + half * 128 + 128] = table
        near = jnp.minimum(apart, 256 - apart).astype(jnp.float32)
        hat = jnp.where(other == 0, jnp.maximum(0.0, 1.0 - near * slope), 0.0).astype(jnp.bfloat16)
        lanes = slice(half * 128, half * 128 + 128)
        hat_ref[grid, rows, lanes] = hat
        hat_ref[grid, pl.ds(pl.multiple_of(256 + step * 32, 32), 32), lanes] = hat


def class_weights(grid, lv_ref, vel_ref):
    m = lv_ref[grid, 1] - 5
    rows = jnp.left_shift(1, m).astype(jnp.float32)
    weights = stencil(vel_ref[grid, 1] * rows * 0.125)
    return [[jnp.where(m == c, w, 0.0) for w in weights] for c in range(4)]


class Sums:
    def __init__(self):
        self.held = {}

    def add(self, offset, number, value):
        key = (offset, number)
        self.held[key] = value if key not in self.held else self.held[key] + value


def spread(blocks, weights, own, up, down):
    for c in range(4):
        centre, behind, ahead = weights[c]
        count = 1 << c
        per = 8 >> c
        for n in range(per):
            w = [blocks[k * per + n] for k in range(count)]
            moved = []
            for k in range(count):
                value = centre * w[k]
                if k > 0:
                    value += behind * w[k - 1]
                if k < count - 1:
                    value += ahead * w[k + 1]
                moved.append(value)
            above, below = behind * w[-1], ahead * w[0]
            line = moved + [above]
            own.add(0, n, moved[0])
            up.add(0, n, above)
            if count == 1:
                down.add(0, n, below)
            for k in range(1, count):
                s = k & -k
                own.add(k * 8 // count, n, line[k] - 0.5 * (line[k - s] + line[k + s]))
            level = 2
            while level <= count:
                up.add(8 // level, n, -0.5 * above)
                spill = -0.5 * moved[0]
                if level == count:
                    spill += below
                down.add(8 - 8 // level, n, spill)
                level *= 2


def contribute(first, weights_row, blocks_ref, at, own_ref, up_ref, down_ref):
    own, up, down = Sums(), Sums(), Sums()
    for grid in range(2):
        blocks = [blocks_ref[at, grid, 8 * n : 8 * n + 8, :] for n in range(8)]
        spread(blocks, weights_of(weights_row, grid), own, up, down)
    for offset, (start, count) in BLOCKS.items():
        for n in range(count):
            low = 8 * (start + n)
            targets = [(own_ref, low, own)]
            if offset in UP:
                targets.append((up_ref, low - UP_ROWS[0], up))
            if offset in DOWN:
                targets.append((down_ref, low - DOWN_ROWS[0], down))
            for ref, row, sums in targets:
                value = sums.held[offset, n]
                ref[row : row + 8, :] = value if first else ref[row : row + 8, :] + value


def weights_of(row, grid):
    return [
        [jnp.broadcast_to(row[:, 12 * grid + 3 * c + n : 12 * grid + 3 * c + n + 1], (8, 128)) for n in range(3)]
        for c in range(4)
    ]


def make_nodes(own_ref, up_ref, down_ref, halo, node_ref, next_ref, back_ref):
    prev_in, up_in, up_far, first_in, down_in, down_far = halo

    def block(ref, n):
        return ref[8 * n : 8 * n + 8, :]

    def held(offset, n):
        at = BLOCKS[offset][0] + n
        value = block(own_ref, at)
        if offset in UP:
            value += block(up_in, at)
        if offset in DOWN:
            value += block(down_in, at - 3)
        return value

    def before(offset, n):
        at = BLOCKS[offset][0] + n - 3
        value = block(prev_in, at) + block(down_ref, at)
        return value + block(up_far, at) if offset in (0, 4) else value

    for n in range(8):
        node = {0: held(0, n), 8: block(first_in, n) + block(up_ref, 3 + n) + block(down_far, n)}
        last = before(0, n)
        back_ref[0, n] = last
        next_ref[n] = node[8]
        node_ref[0, n] = node[0]
        for c in range(1, 4):
            if n >= 8 >> c:
                break
            s = 8 >> c
            for k in range(1, 1 << c, 2):
                node[k * s] = held(k * s, n) + 0.5 * (node[k * s - s] + node[k * s + s])
                node_ref[k * s, n] = node[k * s]
            last = before(8 - s, n) + 0.5 * (last + node[0])
            back_ref[c, n] = last


def interpolate(weights_row, node_ref, next_ref, back_ref, g_ref, at):
    weights = [weights_of(weights_row, grid) for grid in range(2)]
    sums = [Sums(), Sums()]
    for c in range(4):
        per = 8 >> c
        count = 1 << c
        for n in range(per):
            line = [back_ref[c, n]] + [node_ref[k * per, n] for k in range(count)] + [next_ref[n]]
            for k in range(count):
                for grid in range(2):
                    centre, behind, ahead = weights[grid][c]
                    sums[grid].add(
                        0, k * per + n, centre * line[k + 1] + behind * line[k] + ahead * line[k + 2]
                    )
    for grid in range(2):
        for n in range(8):
            g_ref[at, grid, 8 * n : 8 * n + 8, :] = sums[grid].held[0, n]


def kernel(
    nz, nd,
    lv_hbm, vel_hbm, rate_hbm, coef_hbm, v_hbm, s_hbm, out_hbm,
    lv_ref, vel_ref, rate_ref, coef_ref, v_ref, s_ref, left_ref, right_ref, hat_ref,
    w_ref, w_in, row_ref, row_in, own_ref, up_ref, down_ref,
    prev_in, up_in, up_far, first_in, down_in, down_far,
    node_ref, next_ref, back_ref, g_ref, g_in, out_ref,
    small_sem, load_sem, store_sem, w_sem, row_sem, halo_sem, g_sem,
):
    z, d = lax.axis_index("grid"), lax.axis_index("dom")
    small = [
        pltpu.make_async_copy(source, target, small_sem.at[n])
        for n, (source, target) in enumerate(
            ((lv_hbm, lv_ref), (vel_hbm, vel_ref), (rate_hbm, rate_ref), (coef_hbm, coef_ref))
        )
    ]
    for copy in small:
        copy.start()
    loads = []
    for grid in range(2):
        for n, (source, target) in enumerate(((v_hbm, v_ref), (s_hbm, s_ref))):
            loads.append(pltpu.make_async_copy(source.at[grid], target.at[grid], load_sem.at[grid, n]))
            loads[-1].start()

    barrier = pltpu.get_barrier_semaphore()
    peers = [(lax.rem(z + n, nz), d) for n in range(1, nz)]
    peers += [(z, lax.rem(d + n, nd)) for n in (1, 2, nd - 1, nd - 2)]
    for peer in peers:
        pl.semaphore_signal(barrier, inc=1, device_id=peer, device_id_type=MESH)

    def remote(source, target, send, recv, peer):
        return pltpu.make_async_remote_copy(
            src_ref=source, dst_ref=target, send_sem=send, recv_sem=recv, device_id=peer, device_id_type=MESH
        )

    def far_first(i):
        return lax.rem(z + jnp.where(i % 2 == 0, nz // 2 + i // 2, nz // 2 - 1 - (i - 1) // 2), nz)

    for copy in small:
        copy.wait()
    lane = lax.broadcasted_iota(jnp.int32, (1, 128), 1)
    row = jnp.zeros((1, 128), jnp.float32)
    for grid in range(2):
        for c, weights in enumerate(class_weights(grid, lv_ref, vel_ref)):
            for n, weight in enumerate(weights):
                row = jnp.where(lane == 12 * grid + 3 * c + n, weight, row)
    row_ref[...] = row
    for grid in range(2):
        @pl.loop(0, 8)
        def _(step):
            build_tables(grid, step, lv_ref, vel_ref, rate_ref, left_ref, hat_ref)

    for grid in range(2):
        loads[2 * grid].wait()
        loads[2 * grid + 1].wait()
        vh, vl = split(v_ref[grid])
        sh, sl = split(s_ref[grid])
        for slot, part in enumerate((vh, vl, vh, sh, sl)):
            right_ref[grid, :, slot * 256 : slot * 256 + 256] = part
        w = dot(left_ref[grid], right_ref[grid], ((1,), (1,))) * coef_ref[grid].astype(jnp.float32)
        for half in range(2):
            for quarter in range(QUARTERS):
                w_ref[half * QUARTERS + quarter, grid] = w[
                    quarter * 64 : quarter * 64 + 64, half * 128 : half * 128 + 128
                ]

    pl.semaphore_wait(barrier, len(peers))

    def w_copy(slot, target, peer):
        return remote(w_ref.at[peer], w_in.at[slot], w_sem.at[0, peer], w_sem.at[1, slot], (target, d))

    def row_copy(slot, target, peer):
        return remote(row_ref, row_in.at[slot], row_sem.at[0, peer], row_sem.at[1, slot], (target, d))

    @pl.loop(0, nz - 1)
    def _(i):
        peer = far_first(i)
        row_copy(z, peer, peer).start()
        w_copy(z, peer, peer).start()

    contribute(True, row_ref[...], w_ref, z, own_ref, up_ref, down_ref)

    @pl.loop(0, nz - 1)
    def _(i):
        peer = far_first(nz - 2 - i)
        row_copy(peer, peer, peer).wait_recv()
        w_copy(peer, peer, peer).wait_recv()
        contribute(False, row_in[peer], w_in, peer, own_ref, up_ref, down_ref)

    def halo_copy(n, source, target, step):
        return remote(source, target, halo_sem.at[0, n], halo_sem.at[1, n], (z, lax.rem(d + nd + step, nd)))

    halos = [
        halo_copy(0, up_ref.at[24:120, :], up_far, 2),
        halo_copy(1, down_ref.at[0:64, :], down_far, -2),
        halo_copy(2, own_ref.at[24:144, :], prev_in, 1),
        halo_copy(3, own_ref.at[24:88, :], first_in, -1),
        halo_copy(4, up_ref, up_in, 1),
        halo_copy(5, down_ref, down_in, -1),
    ]
    for copy in halos:
        copy.start()
    for copy in halos:
        copy.wait_recv()
    make_nodes(
        own_ref, up_ref, down_ref, (prev_in, up_in, up_far, first_in, down_in, down_far),
        node_ref, next_ref, back_ref,
    )

    def g_copy(slot, target, peer):
        return remote(g_ref.at[peer], g_in.at[slot], g_sem.at[0, peer], g_sem.at[1, slot], (target, d))

    @pl.loop(0, nz - 1)
    def _(i):
        peer = far_first(i)
        interpolate(row_in[peer], node_ref, next_ref, back_ref, g_ref, peer)
        g_copy(z, peer, peer).start()

    interpolate(row_ref[...], node_ref, next_ref, back_ref, g_in, z)

    @pl.loop(0, nz - 1)
    def _(i):
        peer = far_first(nz - 2 - i)
        g_copy(peer, peer, peer).wait_recv()

    stores = []
    for half in range(2):
        for grid in range(2):
            turned = jnp.transpose(
                jnp.concatenate([g_in[half * QUARTERS + n, grid] for n in range(QUARTERS)], axis=0)
            )
            high, low = split(turned)
            lanes = jnp.concatenate([high, low], axis=1)
            rows = slice(half * 128, half * 128 + 128)
            out_ref[grid, rows, :] = dot(lanes, hat_ref[grid], ((1,), (0,)))
            stores.append(
                pltpu.make_async_copy(
                    out_ref.at[grid, rows, :], out_hbm.at[grid, rows, :], store_sem.at[grid, half]
                )
            )
            stores[-1].start()

    for copy in halos:
        copy.wait_send()

    @pl.loop(0, nz - 1)
    def _(i):
        peer = far_first(i)
        row_copy(z, peer, peer).wait_send()
        w_copy(z, peer, peer).wait_send()
        g_copy(z, peer, peer).wait_send()

    for store in stores:
        store.wait()


def local(nz, nd, nodal_values, source_term, velocity, react_rate, levels, comb_coefs):
    f32, bf16 = jnp.float32, jnp.bfloat16
    hbm = pl.BlockSpec(memory_space=pl.ANY)
    sem = pltpu.SemaphoreType.DMA
    return pl.pallas_call(
        functools.partial(kernel, nz, nd),
        out_shape=jax.ShapeDtypeStruct((2, 256, 256), f32),
        in_specs=[hbm] * 6,
        out_specs=hbm,
        scratch_shapes=[
            pltpu.SMEM((2, 2), jnp.int32),
            pltpu.SMEM((2, 2), f32),
            pltpu.SMEM((2,), f32),
            pltpu.SMEM((2,), jnp.int32),
            pltpu.VMEM((2, 256, 256), f32),
            pltpu.VMEM((2, 256, 256), f32),
            pltpu.VMEM((2, 256, KDIM), bf16),
            pltpu.VMEM((2, 256, KDIM), bf16),
            pltpu.VMEM((2, 512, 256), bf16),
            pltpu.VMEM((nz, 2, 64, 128), f32),
            pltpu.VMEM((nz, 2, 64, 128), f32),
            pltpu.VMEM((1, 128), f32),
            pltpu.VMEM((nz, 1, 128), f32),
            pltpu.VMEM((160, 128), f32),
            pltpu.VMEM((120, 128), f32),
            pltpu.VMEM((120, 128), f32),
            pltpu.VMEM((120, 128), f32),
            pltpu.VMEM((120, 128), f32),
            pltpu.VMEM((96, 128), f32),
            pltpu.VMEM((64, 128), f32),
            pltpu.VMEM((120, 128), f32),
            pltpu.VMEM((64, 128), f32),
            pltpu.VMEM((8, 8, 8, 128), f32),
            pltpu.VMEM((8, 8, 128), f32),
            pltpu.VMEM((4, 8, 8, 128), f32),
            pltpu.VMEM((nz, 2, 64, 128), f32),
            pltpu.VMEM((nz, 2, 64, 128), f32),
            pltpu.VMEM((2, 256, 256), f32),
            sem((4,)),
            sem((2, 2)),
            sem((2, 2)),
            sem((2, nz)),
            sem((2, nz)),
            sem((2, 6)),
            sem((2, nz)),
        ],
        compiler_params=pltpu.CompilerParams(collective_id=0, has_side_effects=True, vmem_limit_bytes=67043328),
    )(levels, velocity, react_rate, comb_coefs, nodal_values, source_term)


def solution(mesh):
    in_specs = (
        P("grid", None, "dom"),
        P("grid", None, "dom"),
        P("grid", None),
        P("grid"),
        P("grid", None),
        P("grid"),
    )
    body = functools.partial(local, mesh.shape["grid"], mesh.shape["dom"])
    return jax.shard_map(body, mesh=mesh, in_specs=in_specs, out_specs=P("grid", None, "dom"), check_vma=False)
```

time: 48.6 us -> 45.1 us (0.928)
  the two profiles are of different devices: /device:TPU:1 before, /device:TPU:32 now
where the time goes in v3:
time: 45.1 us; the launch traced here: 44.2 us
  Pallas kernels  42.3 us (94%)
  local copies, waits for them, and re-layouts  1.87 us (4%)
    pallas_call x1, Pallas kernels, local(): pl.pallas_call(functools.partial(kernel, nz, nd), out_shape=jax.ShapeDtyp...  42.3 us
    unnamed x1, local copies, waits for them, and re-layouts  1.87 us

profile of v3, /device:TPU:32, one launch (start us, length us, event | category | flops | bytes accessed | tf_op | source)
XLA Modules:
  0.0 44.2 jit_solution(4256621155133450355)
XLA Ops:
  0.0 42.3 %shard_map.64 = f32[2,256,256]{2,1,0:T(8,128)} custom-call(s32[2,2]{1,0:T(2,128)} %lv_hbm.1, f32[2,2]{1,0:T(2,128)} %vel_hbm.1, f32[2]{0:T(128)} %rate_hbm.1, s32[2]{0:T(128)} %coef_hbm.1, f32[2,256,256]{2,1,0:T(8,128)} %v_hbm.1, f32[2,256,256]{2,1,0:T(8,128)} %s_hbm.1), custom_call_target="tpu_custom_call" | custom-call | tf_op jit(solution)/shard_map/pallas_call | solution.py:378
  42.3 1.9 %copy.8 = f32[2,256,256]{2,1,0:T(8,128)} copy(f32[2,256,256]{2,1,0:T(8,128)} %shard_map.64) | data formatting | bytes 1048576

commit v4 on v3

--- a/solution.py
+++ b/solution.py
@@ -250,8 +250,8 @@
             src_ref=source, dst_ref=target, send_sem=send, recv_sem=recv, device_id=peer, device_id_type=MESH
         )
 
-    def far_first(i):
-        return lax.rem(z + jnp.where(i % 2 == 0, nz // 2 + i // 2, nz // 2 - 1 - (i - 1) // 2), nz)
+    def near_first(i):
+        return lax.rem(z + jnp.where(i % 2 == 0, 1 + i // 2, nz - (i + 1) // 2), nz)
 
     for copy in small:
         copy.wait()
@@ -291,7 +291,7 @@
 
     @pl.loop(0, nz - 1)
     def _(i):
-        peer = far_first(i)
+        peer = near_first(i)
         row_copy(z, peer, peer).start()
         w_copy(z, peer, peer).start()
 
@@ -299,7 +299,7 @@
 
     @pl.loop(0, nz - 1)
     def _(i):
-        peer = far_first(nz - 2 - i)
+        peer = near_first(i)
         row_copy(peer, peer, peer).wait_recv()
         w_copy(peer, peer, peer).wait_recv()
         contribute(False, row_in[peer], w_in, peer, own_ref, up_ref, down_ref)
@@ -327,21 +327,23 @@
     def g_copy(slot, target, peer):
         return remote(g_ref.at[peer], g_in.at[slot], g_sem.at[0, peer], g_sem.at[1, slot], (target, d))
 
-    @pl.loop(0, nz - 1)
-    def _(i):
-        peer = far_first(i)
-        interpolate(row_in[peer], node_ref, next_ref, back_ref, g_ref, peer)
-        g_copy(z, peer, peer).start()
+    @pl.loop(0, nz)
+    def _(peer):
+        @pl.when(peer != z)
+        def _():
+            interpolate(row_in[peer], node_ref, next_ref, back_ref, g_ref, peer)
+            g_copy(z, peer, peer).start()
 
     interpolate(row_ref[...], node_ref, next_ref, back_ref, g_in, z)
-
-    @pl.loop(0, nz - 1)
-    def _(i):
-        peer = far_first(nz - 2 - i)
-        g_copy(peer, peer, peer).wait_recv()
 
     stores = []
     for half in range(2):
+        @pl.loop(half * QUARTERS, half * QUARTERS + QUARTERS)
+        def _(peer):
+            @pl.when(peer != z)
+            def _():
+                g_copy(peer, peer, peer).wait_recv()
+
         for grid in range(2):
             turned = jnp.transpose(
                 jnp.concatenate([g_in[half * QUARTERS + n, grid] for n in range(QUARTERS)], axis=0)
@@ -362,7 +364,7 @@
 
     @pl.loop(0, nz - 1)
     def _(i):
-        peer = far_first(i)
+        peer = near_first(i)
         row_copy(z, peer, peer).wait_send()
         w_copy(z, peer, peer).wait_send()
         g_copy(z, peer, peer).wait_send()

time: 45.1 us -> 42.4 us (0.940)
  the two profiles are of different devices: /device:TPU:32 before, /device:TPU:31 now
where the time goes in v4:
time: 42.4 us; the launch traced here: 42.3 us
  Pallas kernels  40.4 us (95%)
  local copies, waits for them, and re-layouts  1.87 us (4%)
    pallas_call x1, Pallas kernels, local(): pl.pallas_call(functools.partial(kernel, nz, nd), out_shape=jax.ShapeDtyp...  40.4 us
    unnamed x1, local copies, waits for them, and re-layouts  1.87 us

profile of v4, /device:TPU:31, one launch (start us, length us, event | category | flops | bytes accessed | tf_op | source)
XLA Modules:
  0.0 42.3 jit_solution(11033116955660506387)
XLA Ops:
  0.0 40.4 %shard_map.64 = f32[2,256,256]{2,1,0:T(8,128)} custom-call(s32[2,2]{1,0:T(2,128)} %lv_hbm.1, f32[2,2]{1,0:T(2,128)} %vel_hbm.1, f32[2]{0:T(128)} %rate_hbm.1, s32[2]{0:T(128)} %coef_hbm.1, f32[2,256,256]{2,1,0:T(8,128)} %v_hbm.1, f32[2,256,256]{2,1,0:T(8,128)} %s_hbm.1), custom_call_target="tpu_custom_call" | custom-call | tf_op jit(solution)/shard_map/pallas_call | solution.py:380
  40.4 1.9 %copy.8 = f32[2,256,256]{2,1,0:T(8,128)} copy(f32[2,256,256]{2,1,0:T(8,128)} %shard_map.64) | data formatting | bytes 1048576

commit v5 on v4

--- a/solution.py
+++ b/solution.py
@@ -217,12 +217,12 @@
 
 def kernel(
     nz, nd,
-    lv_hbm, vel_hbm, rate_hbm, coef_hbm, v_hbm, s_hbm, out_hbm,
+    lv_hbm, vel_hbm, rate_hbm, coef_hbm, v_hbm, s_hbm, out_ref,
     lv_ref, vel_ref, rate_ref, coef_ref, v_ref, s_ref, left_ref, right_ref, hat_ref,
     w_ref, w_in, row_ref, row_in, own_ref, up_ref, down_ref,
     prev_in, up_in, up_far, first_in, down_in, down_far,
-    node_ref, next_ref, back_ref, g_ref, g_in, out_ref,
-    small_sem, load_sem, store_sem, w_sem, row_sem, halo_sem, g_sem,
+    node_ref, next_ref, back_ref, g_ref, g_in,
+    small_sem, load_sem, w_sem, row_sem, halo_sem, g_sem,
 ):
     z, d = lax.axis_index("grid"), lax.axis_index("dom")
     small = [
@@ -336,7 +336,6 @@
 
     interpolate(row_ref[...], node_ref, next_ref, back_ref, g_in, z)
 
-    stores = []
     for half in range(2):
         @pl.loop(half * QUARTERS, half * QUARTERS + QUARTERS)
         def _(peer):
@@ -352,12 +351,6 @@
             lanes = jnp.concatenate([high, low], axis=1)
             rows = slice(half * 128, half * 128 + 128)
             out_ref[grid, rows, :] = dot(lanes, hat_ref[grid], ((1,), (0,)))
-            stores.append(
-                pltpu.make_async_copy(
-                    out_ref.at[grid, rows, :], out_hbm.at[grid, rows, :], store_sem.at[grid, half]
-                )
-            )
-            stores[-1].start()
 
     for copy in halos:
         copy.wait_send()
@@ -368,9 +361,6 @@
         row_copy(z, peer, peer).wait_send()
         w_copy(z, peer, peer).wait_send()
         g_copy(z, peer, peer).wait_send()
-
-    for store in stores:
-        store.wait()
 
 
 def local(nz, nd, nodal_values, source_term, velocity, react_rate, levels, comb_coefs):
@@ -381,7 +371,7 @@
         functools.partial(kernel, nz, nd),
         out_shape=jax.ShapeDtypeStruct((2, 256, 256), f32),
         in_specs=[hbm] * 6,
-        out_specs=hbm,
+        out_specs=pl.BlockSpec(memory_space=pltpu.VMEM),
         scratch_shapes=[
             pltpu.SMEM((2, 2), jnp.int32),
             pltpu.SMEM((2, 2), f32),
@@ -410,17 +400,15 @@
             pltpu.VMEM((4, 8, 8, 128), f32),
             pltpu.VMEM((nz, 2, 64, 128), f32),
             pltpu.VMEM((nz, 2, 64, 128), f32),
-            pltpu.VMEM((2, 256, 256), f32),
             sem((4,)),
-            sem((2, 2)),
             sem((2, 2)),
             sem((2, nz)),
             sem((2, nz)),
             sem((2, 6)),
             sem((2, nz)),
         ],
-        compiler_params=pltpu.CompilerParams(collective_id=0, has_side_effects=True, vmem_limit_bytes=67043328),
-    )(levels, velocity, react_rate, comb_coefs, nodal_values, source_term)
+        compiler_params=pltpu.CompilerParams(collective_id=0, has_side_effects=True, vmem_limit_bytes=40 << 20),
+    )(*[pltpu.with_memory_space_constraint(x, pltpu.HBM) for x in (levels, velocity, react_rate, comb_coefs, nodal_values, source_term)])
 
 
 def solution(mesh):

time: 42.4 us -> 41.2 us (0.972)
  local copies, waits for them, and re-layouts: 1.87 us -> 0.8 us
    unnamed x1, local copies, waits for them, and re-layouts: 1.87 us -> 0.8 us
where the time goes in v5:
time: 41.2 us; the launch traced here: 41.1 us
  Pallas kernels  40.3 us (98%)
  local copies, waits for them, and re-layouts  0.8 us (2%)
    pallas_call x1, Pallas kernels, local(): pl.pallas_call(functools.partial(kernel, nz, nd), out_shape=jax.ShapeDtyp...  40.3 us

profile of v5, /device:TPU:31, one launch (start us, length us, event | category | flops | bytes accessed | tf_op | source)
XLA Modules:
  0.0 41.1 jit_solution(14069249863589874746)
XLA Ops:
  0.0 40.3 %shard_map.64 = f32[2,256,256]{2,1,0:T(8,128)S(1)} custom-call(s32[2,2]{1,0:T(2,128)} %lv_hbm.1, f32[2,2]{1,0:T(2,128)} %vel_hbm.1, f32[2]{0:T(128)} %rate_hbm.1, s32[2]{0:T(128)} %coef_hbm.1, f32[2,256,256]{2,1,0:T(8,128)} %v_hbm.1, f32[2,256,256]{2,1,0:T(8,128)} %s_hbm.1), custom_call_target="tpu_custom_call" | custom-call | tf_op jit(solution)/shard_map/pallas_call | solution.py:370
  40.3 0.8 %copy.8 = f32[2,256,256]{2,1,0:T(8,128)} copy(f32[2,256,256]{2,1,0:T(8,128)S(1)} %shard_map.64) | data formatting | bytes 1048576

commit v6 on v5

--- a/solution.py
+++ b/solution.py
@@ -14,6 +14,7 @@
 DOWN = (0, 4, 6, 7)
 UP_ROWS = (0, 120)
 DOWN_ROWS = (24, 120)
+SUM_ROWS = 400
 QUARTERS = 4
 FAR = 1 << 20
 KDIM = 1280
@@ -134,7 +135,11 @@
                 level *= 2
 
 
-def contribute(first, weights_row, blocks_ref, at, own_ref, up_ref, down_ref):
+def own_row(low):
+    return 360 + low if low < 24 else 96 + low if low < 144 else 240 + low
+
+
+def contribute(first, weights_row, blocks_ref, at, sums_ref):
     own, up, down = Sums(), Sums(), Sums()
     for grid in range(2):
         blocks = [blocks_ref[at, grid, 8 * n : 8 * n + 8, :] for n in range(8)]
@@ -142,14 +147,14 @@
     for offset, (start, count) in BLOCKS.items():
         for n in range(count):
             low = 8 * (start + n)
-            targets = [(own_ref, low, own)]
+            targets = [(own_row(low), own)]
             if offset in UP:
-                targets.append((up_ref, low - UP_ROWS[0], up))
+                targets.append((240 + low - UP_ROWS[0], up))
             if offset in DOWN:
-                targets.append((down_ref, low - DOWN_ROWS[0], down))
-            for ref, row, sums in targets:
+                targets.append((low - DOWN_ROWS[0], down))
+            for row, sums in targets:
                 value = sums.held[offset, n]
-                ref[row : row + 8, :] = value if first else ref[row : row + 8, :] + value
+                sums_ref[row : row + 8, :] = value if first else sums_ref[row : row + 8, :] + value
 
 
 def weights_of(row, grid):
@@ -159,28 +164,28 @@
     ]
 
 
-def make_nodes(own_ref, up_ref, down_ref, halo, node_ref, next_ref, back_ref):
-    prev_in, up_in, up_far, first_in, down_in, down_far = halo
-
-    def block(ref, n):
-        return ref[8 * n : 8 * n + 8, :]
+def make_nodes(sums_ref, halo, node_ref, next_ref, back_ref):
+    after_in, before_in, up_far, down_far = halo
+
+    def block(ref, n, start=0):
+        return ref[start + 8 * n : start + 8 * n + 8, :]
 
     def held(offset, n):
         at = BLOCKS[offset][0] + n
-        value = block(own_ref, at)
+        value = block(sums_ref, 0, own_row(8 * at))
         if offset in UP:
-            value += block(up_in, at)
+            value += block(after_in, at, 120)
         if offset in DOWN:
-            value += block(down_in, at - 3)
+            value += block(before_in, at - 3)
         return value
 
     def before(offset, n):
         at = BLOCKS[offset][0] + n - 3
-        value = block(prev_in, at) + block(down_ref, at)
+        value = block(after_in, at) + block(sums_ref, at)
         return value + block(up_far, at) if offset in (0, 4) else value
 
     for n in range(8):
-        node = {0: held(0, n), 8: block(first_in, n) + block(up_ref, 3 + n) + block(down_far, n)}
+        node = {0: held(0, n), 8: block(before_in, n, 120) + block(sums_ref, 3 + n, 240) + block(down_far, n)}
         last = before(0, n)
         back_ref[0, n] = last
         next_ref[n] = node[8]
@@ -219,8 +224,8 @@
     nz, nd,
     lv_hbm, vel_hbm, rate_hbm, coef_hbm, v_hbm, s_hbm, out_ref,
     lv_ref, vel_ref, rate_ref, coef_ref, v_ref, s_ref, left_ref, right_ref, hat_ref,
-    w_ref, w_in, row_ref, row_in, own_ref, up_ref, down_ref,
-    prev_in, up_in, up_far, first_in, down_in, down_far,
+    w_ref, w_in, row_ref, row_in, sums_ref,
+    after_in, before_in, up_far, down_far,
     node_ref, next_ref, back_ref, g_ref, g_in,
     small_sem, load_sem, w_sem, row_sem, halo_sem, g_sem,
 ):
@@ -295,40 +300,39 @@
         row_copy(z, peer, peer).start()
         w_copy(z, peer, peer).start()
 
-    contribute(True, row_ref[...], w_ref, z, own_ref, up_ref, down_ref)
+    contribute(True, row_ref[...], w_ref, z, sums_ref)
 
     @pl.loop(0, nz - 1)
     def _(i):
         peer = near_first(i)
         row_copy(peer, peer, peer).wait_recv()
         w_copy(peer, peer, peer).wait_recv()
-        contribute(False, row_in[peer], w_in, peer, own_ref, up_ref, down_ref)
+        contribute(False, row_in[peer], w_in, peer, sums_ref)
 
     def halo_copy(n, source, target, step):
         return remote(source, target, halo_sem.at[0, n], halo_sem.at[1, n], (z, lax.rem(d + nd + step, nd)))
 
     halos = [
-        halo_copy(0, up_ref.at[24:120, :], up_far, 2),
-        halo_copy(1, down_ref.at[0:64, :], down_far, -2),
-        halo_copy(2, own_ref.at[24:144, :], prev_in, 1),
-        halo_copy(3, own_ref.at[24:88, :], first_in, -1),
-        halo_copy(4, up_ref, up_in, 1),
-        halo_copy(5, down_ref, down_in, -1),
+        halo_copy(0, sums_ref.at[264:360, :], up_far, 2),
+        halo_copy(1, sums_ref.at[0:64, :], down_far, -2),
+        halo_copy(2, sums_ref.at[120:360, :], after_in, 1),
+        halo_copy(3, sums_ref.at[0:184, :], before_in, -1),
     ]
     for copy in halos:
         copy.start()
     for copy in halos:
         copy.wait_recv()
     make_nodes(
-        own_ref, up_ref, down_ref, (prev_in, up_in, up_far, first_in, down_in, down_far),
-        node_ref, next_ref, back_ref,
+        sums_ref, (after_in, before_in, up_far, down_far), node_ref, next_ref, back_ref,
     )
 
     def g_copy(slot, target, peer):
         return remote(g_ref.at[peer], g_in.at[slot], g_sem.at[0, peer], g_sem.at[1, slot], (target, d))
 
     @pl.loop(0, nz)
-    def _(peer):
+    def _(i):
+        peer = jnp.where(i % 4 == 1, i + 1, jnp.where(i % 4 == 2, i - 1, i))
+
         @pl.when(peer != z)
         def _():
             interpolate(row_in[peer], node_ref, next_ref, back_ref, g_ref, peer)
@@ -386,14 +390,10 @@
             pltpu.VMEM((nz, 2, 64, 128), f32),
             pltpu.VMEM((1, 128), f32),
             pltpu.VMEM((nz, 1, 128), f32),
-            pltpu.VMEM((160, 128), f32),
-            pltpu.VMEM((120, 128), f32),
-            pltpu.VMEM((120, 128), f32),
-            pltpu.VMEM((120, 128), f32),
-            pltpu.VMEM((120, 128), f32),
+            pltpu.VMEM((SUM_ROWS, 128), f32),
+            pltpu.VMEM((240, 128), f32),
+            pltpu.VMEM((184, 128), f32),
             pltpu.VMEM((96, 128), f32),
-            pltpu.VMEM((64, 128), f32),
-            pltpu.VMEM((120, 128), f32),
             pltpu.VMEM((64, 128), f32),
             pltpu.VMEM((8, 8, 8, 128), f32),
             pltpu.VMEM((8, 8, 128), f32),
@@ -404,7 +404,7 @@
             sem((2, 2)),
             sem((2, nz)),
             sem((2, nz)),
-            sem((2, 6)),
+            sem((2, 4)),
             sem((2, nz)),
         ],
         compiler_params=pltpu.CompilerParams(collective_id=0, has_side_effects=True, vmem_limit_bytes=40 << 20),

time: 41.2 us -> 40.8 us (level)
  the two profiles are of different devices: /device:TPU:31 before, /device:TPU:32 now
where the time goes in v6:
time: 40.8 us; the launch traced here: 40.7 us
  Pallas kernels  39.9 us (98%)
  local copies, waits for them, and re-layouts  0.8 us (2%)
    pallas_call x1, Pallas kernels, local(): pl.pallas_call(functools.partial(kernel, nz, nd), out_shape=jax.ShapeDtyp...  39.9 us

profile of v6, /device:TPU:32, one launch (start us, length us, event | category | flops | bytes accessed | tf_op | source)
XLA Modules:
  0.0 40.7 jit_solution(13213680566633909681)
XLA Ops:
  0.0 39.9 %shard_map.64 = f32[2,256,256]{2,1,0:T(8,128)S(1)} custom-call(s32[2,2]{1,0:T(2,128)} %lv_hbm.1, f32[2,2]{1,0:T(2,128)} %vel_hbm.1, f32[2]{0:T(128)} %rate_hbm.1, s32[2]{0:T(128)} %coef_hbm.1, f32[2,256,256]{2,1,0:T(8,128)} %v_hbm.1, f32[2,256,256]{2,1,0:T(8,128)} %s_hbm.1), custom_call_target="tpu_custom_call" | custom-call | tf_op jit(solution)/shard_map/pallas_call | solution.py:374
  39.9 0.8 %copy.8 = f32[2,256,256]{2,1,0:T(8,128)} copy(f32[2,256,256]{2,1,0:T(8,128)S(1)} %shard_map.64) | data formatting | bytes 1048576

commit v7 on v6

--- a/solution.py
+++ b/solution.py
@@ -331,7 +331,7 @@
 
     @pl.loop(0, nz)
     def _(i):
-        peer = jnp.where(i % 4 == 1, i + 1, jnp.where(i % 4 == 2, i - 1, i))
+        peer = jnp.where(i < 3, lax.rem(i + 2, 3), jnp.where(i == 5, 6, jnp.where(i == 6, 5, i)))
 
         @pl.when(peer != z)
         def _():

time: 40.8 us -> 40.6 us (level)
  no operation moved by 1% of the time
where the time goes in v7:
time: 40.6 us; the launch traced here: 40.5 us
  Pallas kernels  39.7 us (98%)
  local copies, waits for them, and re-layouts  0.8 us (2%)
    pallas_call x1, Pallas kernels, local(): pl.pallas_call(functools.partial(kernel, nz, nd), out_shape=jax.ShapeDtyp...  39.7 us

profile of v7, /device:TPU:32, one launch (start us, length us, event | category | flops | bytes accessed | tf_op | source)
XLA Modules:
  0.0 40.5 jit_solution(11104172609000436045)
XLA Ops:
  0.0 39.7 %shard_map.64 = f32[2,256,256]{2,1,0:T(8,128)S(1)} custom-call(s32[2,2]{1,0:T(2,128)} %lv_hbm.1, f32[2,2]{1,0:T(2,128)} %vel_hbm.1, f32[2]{0:T(128)} %rate_hbm.1, s32[2]{0:T(128)} %coef_hbm.1, f32[2,256,256]{2,1,0:T(8,128)} %v_hbm.1, f32[2,256,256]{2,1,0:T(8,128)} %s_hbm.1), custom_call_target="tpu_custom_call" | custom-call | tf_op jit(solution)/shard_map/pallas_call | solution.py:374
  39.7 0.8 %copy.8 = f32[2,256,256]{2,1,0:T(8,128)} copy(f32[2,256,256]{2,1,0:T(8,128)S(1)} %shard_map.64) | data formatting | bytes 1048576

commit v8 on v7

--- a/solution.py
+++ b/solution.py
@@ -256,7 +256,7 @@
         )
 
     def near_first(i):
-        return lax.rem(z + jnp.where(i % 2 == 0, 1 + i // 2, nz - (i + 1) // 2), nz)
+        return lax.rem(z + jnp.where((i + d) % 2 == 0, 1 + i // 2, nz - 1 - i // 2), nz)
 
     for copy in small:
         copy.wait()

time: 40.6 us -> 40.6 us (level)
  no operation moved by 1% of the time
where the time goes in v8:
time: 40.6 us; the launch traced here: 40.5 us
  Pallas kernels  39.7 us (98%)
  local copies, waits for them, and re-layouts  0.8 us (2%)
    pallas_call x1, Pallas kernels, local(): pl.pallas_call(functools.partial(kernel, nz, nd), out_shape=jax.ShapeDtyp...  39.7 us

profile of v8, /device:TPU:32, one launch (start us, length us, event | category | flops | bytes accessed | tf_op | source)
XLA Modules:
  0.0 40.5 jit_solution(6574194705973061061)
XLA Ops:
  0.0 39.7 %shard_map.64 = f32[2,256,256]{2,1,0:T(8,128)S(1)} custom-call(s32[2,2]{1,0:T(2,128)} %lv_hbm.1, f32[2,2]{1,0:T(2,128)} %vel_hbm.1, f32[2]{0:T(128)} %rate_hbm.1, s32[2]{0:T(128)} %coef_hbm.1, f32[2,256,256]{2,1,0:T(8,128)} %v_hbm.1, f32[2,256,256]{2,1,0:T(8,128)} %s_hbm.1), custom_call_target="tpu_custom_call" | custom-call | tf_op jit(solution)/shard_map/pallas_call | solution.py:374
  39.7 0.8 %copy.8 = f32[2,256,256]{2,1,0:T(8,128)} copy(f32[2,256,256]{2,1,0:T(8,128)S(1)} %shard_map.64) | data formatting | bytes 1048576
